TPU v7x, 128 devices: a whole 4x4x4 slice. The times are simulated.
128 devices in a mesh: dp: 2 (over y_lo), ctx: 64 (over x, y_hi, z, core).
Axes of the slice: x: 4, y: 4 (y_hi: 2, y_lo: 2; y = y_hi * 2 + y_lo), z: 4, core: 2. Of those that a mesh axis runs over, the one named last changes fastest.
Arguments:
- tokens: bfloat16 [2, 24576, 2560], P('dp', 'ctx'), may hold values from -32 to 32
- qkv_weight: bfloat16 [2560, 3840], P(None, 'dp'), may hold values from -8 to 8
- out_weight: bfloat16 [1280, 2560], P(None, 'dp'), may hold values from -3.5 to 3.5
- offsets: int32 [4, 10], replicated, may hold values from 0 to 7, as said below
Outputs:
- mixed: bfloat16 [2, 24576, 2560], P('dp', 'ctx')
Inputs may be any that keep to these rules, and one draw needn't show every extreme that they name: offsets[j, h] is at most 2 ** j - 1 for level j.
All inputs are finite; a program needn't handle non-finite values.
Results may differ from a plain program's by a relative error of at most 0.0083.
Values may be sent and summed in bfloat16 or wider, within the bound.
No kernel may reach another device: no remote copies, remote signals or barrier semaphores. Data moves between devices by JAX's collectives and lax.ppermute only.
A program may use at most 192 MiB of HBM per device.

v0:
```python
import jax
import jax.numpy as jnp
from jax import lax
from jax.sharding import PartitionSpec as P


def from_partner(block, axis, stride):
    count = lax.axis_size(axis)
    route = []
    for low in range(count):
        high = low | 1 << stride
        if high != low and high < count:
            route += [(low, high), (high, low)]
    return lax.ppermute(block, axis, route)


def pick_table(offset_row, dilation):
    return jnp.arange(dilation, dtype=jnp.int32)[:, None] == offset_row[None, :]


def select_rows(values_in, chosen, dilation):
    array_shape = values_in.shape
    grouped = values_in.reshape((array_shape[0] // dilation, dilation) + array_shape[1:])
    middle_dims = len(array_shape) - 3
    table = chosen.reshape((1, dilation) + (1,) * middle_dims + (chosen.shape[1], 1))
    return jnp.sum(jnp.where(table, grouped, jnp.zeros((), grouped.dtype)), axis=1)


def attend(queries, key_rows, value_rows, score_scale):
    scores = (
        jnp.einsum("qhd,khd->hqk", queries, key_rows, preferred_element_type=jnp.float32)
        * score_scale
    )
    row_max = jnp.max(scores, axis=2, keepdims=True)
    expo = jnp.exp(scores - row_max)
    row_total = jnp.sum(expo, axis=2)
    blended = jnp.einsum(
        "hqk,khd->qhd", expo.astype(jnp.bfloat16), value_rows, preferred_element_type=jnp.float32
    )
    return (blended / row_total.T[:, :, None], (row_max[:, :, 0] + jnp.log(row_total)).T)


def local(tokens, qkv_weight, out_weight, offsets):
    tok_rows = tokens.shape[1]
    level_count = offsets.shape[0]
    head_count = offsets.shape[1]
    inner_width = out_weight.shape[0]
    head_size = inner_width // head_count
    token_flat = tokens.reshape(tok_rows, tokens.shape[2])
    projected = jnp.dot(
        token_flat,
        lax.all_gather(qkv_weight, "dp", axis=1, tiled=True),
        preferred_element_type=jnp.float32,
    ).astype(jnp.bfloat16)
    all_query = projected[:, :inner_width].reshape(tok_rows, head_count, head_size)
    keyval = projected[:, inner_width:].reshape(tok_rows, 2, head_count, head_size)
    pick_tables = [pick_table(offsets[degree], 2**degree) for degree in range(level_count)]
    queries = [
        select_rows(all_query, pick_tables[degree], 2**degree) for degree in range(level_count)
    ]
    pieces = [
        select_rows(keyval, pick_tables[degree], 2**degree).reshape(
            tok_rows // 2**degree, 2, inner_width
        )
        for degree in range(level_count)
    ]
    bit_order = list(range(level_count))
    collected = []
    for degree in range(level_count):
        gathered = pieces[degree]
        for which_bit in bit_order:
            if which_bit <= degree:
                partner = from_partner(gathered, "ctx", which_bit)
                gathered = jnp.concatenate([gathered, partner], axis=0)
        collected.append(gathered)
    score_scale = head_size ** (-0.5)
    for degree in range(level_count):
        key_rows = collected[degree][:, 0].reshape(-1, head_count, head_size)
        value_rows = collected[degree][:, 1].reshape(-1, head_count, head_size)
        blended, row_lse = attend(queries[degree], key_rows, value_rows, score_scale)
        chosen = pick_tables[degree][None, :, :]
        level_out = jnp.where(chosen[..., None], blended[:, None], 0.0).reshape(
            tok_rows, head_count, head_size
        )
        level_lse = jnp.where(chosen, row_lse[:, None], -jnp.inf).reshape(tok_rows, head_count)
        if degree == 0:
            weighted = level_out
            totals = jnp.ones_like(level_lse)
            running = level_lse
        else:
            newest = jnp.maximum(running, level_lse)
            former = jnp.exp(running - newest)
            fresh = jnp.exp(level_lse - newest)
            weighted = weighted * former[..., None] + fresh[..., None] * level_out
            totals = totals * former + fresh
            running = newest
    attended = (weighted / totals[..., None]).astype(jnp.bfloat16).reshape(tok_rows, inner_width)
    mixed = jnp.dot(
        attended,
        lax.all_gather(out_weight, "dp", axis=1, tiled=True),
        preferred_element_type=jnp.float32,
    ).astype(jnp.bfloat16)
    return mixed.reshape(1, tok_rows, mixed.shape[1])


def solution(mesh):
    in_specs = (P("dp", "ctx", None), P(None, "dp"), P(None, "dp"), P())
    out_specs = P("dp", "ctx", None)
    return jax.shard_map(local, mesh=mesh, in_specs=in_specs, out_specs=out_specs, check_vma=False)
```

profile of v0, /device:TPU:0, one launch (start us, length us, event | category | flops | bytes accessed | tf_op | source)
XLA Modules:
  0.0 501.0 jit_solution(6811902256076072925)
XLA Ops:
  8.9 238.1 %all-gather.3.cloned.1.call-done = bf16[2560,3840]{1,0:T(8,128)(2,1)} async-done(((bf16[2560,1920]{1,0:T(8,128)(2,1)}), bf16[2560,3840]{1,0:T(8,128)(2,1)}) %all-gather.3.cloned.1.call-update) | async-done | bytes 19660816 | tf_op jit(solution)/shard_map/all_gather | solution.py:52
  247.0 12.3 %convolution_convert_fusion = bf16[384,3840]{1,0:T(8,128)(2,1)S(1)} fusion(bf16[2560,3840]{1,0:T(8,128)(2,1)} %all-gather.3.cloned.1.call-done, bf16[1,384,2560]{2,1,0:T(8,128)(2,1)S(1)} %copy-done), kind=kOutput, calls=%fused_computation.8 | convolution fusion | flops 7551221760 | bytes 24576000 | tf_op jit(solution)/shard_map/dot_general | solution.py:50
  261.0 2.7 reshape_reshape.27
  263.8 2.7 reshape_reshape.29
  266.5 2.9 fusion.41
  269.4 2.3 copy.120
  274.4 4.9 select_reduce_fusion.1
  279.4 2.0 copy.74
  282.8 4.2 select_reduce_fusion
  286.9 2.6 copy.87
  289.5 2.1 copy.88
  292.5 2.1 select_reduce_fusion.2
  296.5 3.2 broadcast_select_fusion
  301.2 3.4 select_reduce_fusion.4
  306.0 1.6 collective-permute-start.7
  310.4 1.6 pad_maximum_fusion.6
  312.0 2.3 copy.90
  314.8 5.5 %collective-permute-done.7 = bf16[96,2,1280]{2,0,1:T(8,128)(2,1)S(1)} collective-permute-done((bf16[96,2,1280]{2,0,1:T(8,128)(2,1)}, bf16[96,2,1280]{2,0,1:T(8,128)(2,1)S(1)}, u32[]{:S(2)}, u32[]{:S(2)}) %collective-permute-start.7) | collective-permute-done | bytes 491552 | tf_op jit(solution)/shard_map/ppermute | solution.py:14
  320.3 2.2 pad_maximum_fusion.7
  322.5 3.2 collective-permute-start.8
  327.2 1.5 copy.77
  328.7 2.0 pad_maximum_fusion.3
  331.4 10.1 %collective-permute-done.4 = bf16[192,2,1280]{2,0,1:T(8,128)(2,1)} collective-permute-done((bf16[192,2,1280]{2,0,1:T(8,128)(2,1)}, bf16[192,2,1280]{2,0,1:T(8,128)(2,1)}, u32[]{:S(2)}, u32[]{:S(2)}) %collective-permute-start.4) | collective-permute-done | bytes 983072 | tf_op jit(solution)/shard_map/ppermute | solution.py:14
  343.1 3.5 pad_maximum_fusion.4
  346.6 3.2 collective-permute-start.5
  349.7 15.2 %collective-permute-done.8 = bf16[192,2,1280]{2,0,1:T(8,128)(2,1)} collective-permute-done((bf16[192,2,1280]{2,0,1:T(8,128)(2,1)}, bf16[192,2,1280]{2,0,1:T(8,128)(2,1)}, u32[]{:S(2)}, u32[]{:S(2)}) %collective-permute-start.8) | collective-permute-done | bytes 983072 | tf_op jit(solution)/shard_map/ppermute | solution.py:14
  365.0 2.6 pad_maximum_fusion.5
  367.6 2.7 collective-permute-start.9
  370.3 2.3 constant_dynamic-update-slice_fusion.1
  372.5 3.5 pad_maximum_fusion.2
  376.0 1.9 multiply_reduce_fusion
  378.0 2.7 fusion
  380.7 1.6 copy-done.2
  382.3 22.4 %collective-permute-done.2 = bf16[384,2,1280]{0,2,1:T(8,128)(2,1)} collective-permute-done((bf16[384,2,1280]{0,2,1:T(8,128)(2,1)}, bf16[384,2,1280]{0,2,1:T(8,128)(2,1)}, u32[]{:S(2)}, u32[]{:S(2)}) %collective-permute-start.2) | collective-permute-done | bytes 1966112 | tf_op jit(solution)/shard_map/ppermute | solution.py:14
  404.7 2.7 pad_maximum_fusion
  410.9 1.6 fusion.45
  413.4 2.2 copy.141
  415.5 2.9 copy.86
  418.7 29.5 %collective-permute-done.5 = bf16[384,2,1280]{0,2,1:T(8,128)(2,1)} collective-permute-done((bf16[384,2,1280]{0,2,1:T(8,128)(2,1)}, bf16[384,2,1280]{0,2,1:T(8,128)(2,1)}, u32[]{:S(2)}, u32[]{:S(2)}) %collective-permute-start.5) | collective-permute-done | bytes 1966112 | tf_op jit(solution)/shard_map/ppermute | solution.py:14
  448.2 3.5 pad_maximum_fusion.1
  456.9 1.8 copy.103
  459.0 3.0 constant_dynamic-update-slice_fusion
  462.0 4.4 fusion.67
  466.4 2.7 copy.105
  469.1 4.1 copy.108
  475.8 1.8 copy.111
  478.0 7.8 %fusion.21 = f32[384,10,128]{0,2,1:T(8,128)S(1)} fusion(bf16[768,10,128]{0,2,1:T(8,128)(2,1)} %bitcast.162, f32[10,384,768]{2,1,0:T(8,128)} %copy-done.2, f32[10,384]{1,0:T(8,128)S(1)} %get-tuple-element.25, f32[384,10]{0,1:T(8,128)S(1)} %get-tuple-element.11, f32[384,10]{0,1:T(8,128)S(1)} %bitcast.168, pred[10]{0:T(512)(128)(4,1)S(1)} %compare_bitcast_fusion), kind=kOutput, calls=%fused_computation.46 | convolution fusion | flops 765296640 | bytes 15774730 | tf_op jit(solution)/shard_map/hqk,khd->qhd/dot_general | solution.py:37
  486.9 7.0 %fusion.8 = bf16[1,384,2560]{2,1,0:T(8,128)(2,1)} fusion(bf16[384,1280]{0,1:T(8,128)(2,1)S(1)} %fusion.16, bf16[1280,2560]{1,0:T(8,128)(2,1)} %all-gather.5.cloned.1.call-done), kind=kOutput, calls=%fused_computation.17 | convolution fusion | flops 2517565440 | bytes 9502720 | tf_op jit(solution)/shard_map/dot_general | solution.py:98
  (132 shorter events, 35.0 us)
Async XLA Ops:
  6.5 240.4 %copy-start = (bf16[1,384,2560]{2,1,0:T(8,128)(2,1)S(1)}, bf16[1,384,2560]{2,1,0:T(8,128)(2,1)}, u32[]{:S(2)}) copy-start(bf16[1,384,2560]{2,1,0:T(8,128)(2,1)} %param.4) | copy-start | bytes 5898244
  6.5 240.4 %all-gather.3.cloned.1.call-start = ((), (), s32[]{:S(2)}) async-start(), calls=%async_computation | async-start | bytes 29491200 | tf_op jit(solution)/shard_map/all_gather | solution.py:52
  7.3 0.8 copy-start.29
  7.3 479.6 %all-gather.5.cloned.1.call-start = ((), (), s32[]{:S(2)}) async-start(), calls=%async_computation.1 | async-start | bytes 9830400 | tf_op jit(solution)/shard_map/all_gather | solution.py:100
  8.1 266.4 %copy-start.27 = (pred[2,10]{1,0:T(4,128)(4,1)}, pred[2,10]{1,0:T(4,128)(4,1)S(1)}, u32[]{:S(2)}) copy-start(pred[2,10]{1,0:T(4,128)(4,1)S(1)} %iota_compare_fusion.2) | copy-start | bytes 64
  8.1 274.7 %copy-start.25 = (pred[4,10]{1,0:T(4,128)(4,1)}, pred[4,10]{1,0:T(4,128)(4,1)S(1)}, u32[]{:S(2)}) copy-start(pred[4,10]{1,0:T(4,128)(4,1)S(1)} %iota_compare_fusion.1) | copy-start | bytes 124
  259.3 1.6 copy-start.14
  261.0 12.1 %copy-start.4 = (bf16[384,1280]{1,0:T(8,128)(2,1)}, bf16[384,1280]{1,0:T(8,128)(2,1)S(1)}, u32[]{:S(2)}) copy-start(bf16[384,1280]{1,0:T(8,128)(2,1)S(1)} %slice.68) | copy-start | bytes 2949124
  282.8 44.4 %collective-permute-start.1 = (bf16[192,2,1280]{2,0,1:T(8,128)(2,1)}, bf16[192,2,1280]{2,0,1:T(8,128)(2,1)}, u32[]{:S(2)}, u32[]{:S(2)}) collective-permute-start(bf16[192,2,1280]{2,0,1:T(8,128)(2,1)} %copy.75), channel_id=1, source_target_pairs={{0,1},{1,0},{2,3},{3,2},{4,5},{5,4},{6,7},{7,6},{8,9},{9,8},{10,11... | collective-permute-start | bytes 2949128 | tf_op jit(solution)/shard_map/ppermute | solution.py:14
  291.6 17.4 %collective-permute-start.3 = (bf16[96,2,1280]{2,0,1:T(8,128)(2,1)}, bf16[96,2,1280]{2,0,1:T(8,128)(2,1)}, u32[]{:S(2)}, u32[]{:S(2)}) collective-permute-start(bf16[96,2,1280]{2,0,1:T(8,128)(2,1)} %copy.88), channel_id=1, source_target_pairs={{0,1},{1,0},{2,3},{3,2},{4,5},{5,4},{6,7},{7,6},{8,9},{9,8},{10,11... | collective-permute-start | bytes 1474568 | tf_op jit(solution)/shard_map/ppermute | solution.py:14
  296.5 8.7 %collective-permute-start.6 = (bf16[48,2,1280]{2,0,1:T(8,128)(2,1)S(1)}, bf16[48,2,1280]{2,0,1:T(8,128)(2,1)S(1)}, u32[]{:S(2)}, u32[]{:S(2)}) collective-permute-start(bf16[48,2,1280]{2,0,1:T(8,128)(2,1)S(1)} %get-tuple-element.20), channel_id=1, source_target_pairs={{0,1},{1,0},{2,3},{3,2},{4,5},{5,4},{6,7},{7,6},{8,9},{9,8},{10,11... | collective-permute-start | bytes 737288 | tf_op jit(solution)/shard_map/ppermute | solution.py:14
  296.5 3.2 copy-start.5
  299.7 1.5 copy-start.28
  301.2 6.3 %copy-start.13 = (bf16[96,4,10,128]{3,2,1,0:T(8,128)(2,1)S(1)}, bf16[96,4,10,128]{3,2,1,0:T(8,128)(2,1)}, u32[]{:S(2)}) copy-start(bf16[96,4,10,128]{3,2,1,0:T(8,128)(2,1)} %reshape_reshape.28) | copy-start | bytes 2949124
  301.2 6.3 %copy-start.26 = (pred[4,10]{1,0:T(4,128)(4,1)S(1)}, pred[4,10]{1,0:T(4,128)(4,1)}, u32[]{:S(2)}) copy-start(pred[4,10]{1,0:T(4,128)(4,1)} %copy-done.25) | copy-start | bytes 124
  304.6 5.7 %copy-start.3 = (bf16[96,2,10,128]{0,3,2,1:T(8,128)(2,1)S(1)}, bf16[96,2,10,128]{0,3,2,1:T(8,128)(2,1)}, u32[]{:S(2)}) copy-start(bf16[96,2,10,128]{0,3,2,1:T(8,128)(2,1)} %copy.87) | copy-start | bytes 1474564
  304.7 67.9 %collective-permute-start = (bf16[384,2,1280]{0,2,1:T(8,128)(2,1)}, bf16[384,2,1280]{0,2,1:T(8,128)(2,1)}, u32[]{:S(2)}, u32[]{:S(2)}) collective-permute-start(bf16[384,2,1280]{0,2,1:T(8,128)(2,1)} %broadcast_select_fusion), channel_id=1, source_target_pairs={{0,1},{1,0},{2,3},{3,2},{4,5},{5,4},{6,7},{7,6},{8,9},{9,8},{10,11... | collective-permute-start | bytes 5898248 | tf_op jit(solution)/shard_map/ppermute | solution.py:14
  305.1 3.9 copy-start.18
  306.0 14.3 %collective-permute-start.7 = (bf16[96,2,1280]{2,0,1:T(8,128)(2,1)}, bf16[96,2,1280]{2,0,1:T(8,128)(2,1)S(1)}, u32[]{:S(2)}, u32[]{:S(2)}) collective-permute-start(bf16[96,2,1280]{2,0,1:T(8,128)(2,1)} %pad_maximum_fusion.8), channel_id=1, source_target_pairs={{0,2},{2,0},{1,3},{3,1},{4,6},{6,4},{5,7},{7,5},{8,10},{10,8},{9,1... | collective-permute-start | bytes 1474568 | tf_op jit(solution)/shard_map/ppermute | solution.py:14
  310.4 4.0 copy-start.8
  314.4 11.3 %copy-start.19 = (bf16[48,2,1280]{2,0,1:T(8,128)(2,1)S(1)}, bf16[48,2,1280]{2,0,1:T(8,128)(2,1)}, u32[]{:S(2)}) copy-start(bf16[48,2,1280]{2,0,1:T(8,128)(2,1)} %copy-done.18) | copy-start | bytes 737284
  314.4 27.1 %collective-permute-start.4 = (bf16[192,2,1280]{2,0,1:T(8,128)(2,1)}, bf16[192,2,1280]{2,0,1:T(8,128)(2,1)}, u32[]{:S(2)}, u32[]{:S(2)}) collective-permute-start(bf16[192,2,1280]{2,0,1:T(8,128)(2,1)} %copy.90), channel_id=1, source_target_pairs={{0,2},{2,0},{1,3},{3,1},{4,6},{6,4},{5,7},{7,5},{8,10},{10,8},{9,1... | collective-permute-start | bytes 2949128 | tf_op jit(solution)/shard_map/ppermute | solution.py:14
  320.3 6.9 %copy-start.15 = (bf16[96,2,1280]{2,0,1:T(8,128)(2,1)}, bf16[96,2,1280]{2,0,1:T(8,128)(2,1)S(1)}, u32[]{:S(2)}) copy-start(bf16[96,2,1280]{2,0,1:T(8,128)(2,1)S(1)} %collective-permute-done.7) | copy-start | bytes 1474564
  322.5 42.5 %collective-permute-start.8 = (bf16[192,2,1280]{2,0,1:T(8,128)(2,1)}, bf16[192,2,1280]{2,0,1:T(8,128)(2,1)}, u32[]{:S(2)}, u32[]{:S(2)}) collective-permute-start(bf16[192,2,1280]{2,0,1:T(8,128)(2,1)} %pad_maximum_fusion.7), channel_id=1, source_target_pairs={{0,4},{4,0},{1,5},{5,1},{2,6},{6,2},{3,7},{7,3},{8,12},{12,8},{9,1... | collective-permute-start | bytes 2949128 | tf_op jit(solution)/shard_map/ppermute | solution.py:14
  328.7 2.0 copy-start.6
  330.8 73.9 %collective-permute-start.2 = (bf16[384,2,1280]{0,2,1:T(8,128)(2,1)}, bf16[384,2,1280]{0,2,1:T(8,128)(2,1)}, u32[]{:S(2)}, u32[]{:S(2)}) collective-permute-start(bf16[384,2,1280]{0,2,1:T(8,128)(2,1)} %pad_maximum_fusion.3), channel_id=1, source_target_pairs={{0,2},{2,0},{1,3},{3,1},{4,6},{6,4},{5,7},{7,5},{8,10},{10,8},{9,1... | collective-permute-start | bytes 5898248 | tf_op jit(solution)/shard_map/ppermute | solution.py:14
  343.0 21.9 %copy-start.16 = (bf16[96,2,1280]{2,0,1:T(8,128)(2,1)S(1)}, bf16[96,2,1280]{2,0,1:T(8,128)(2,1)}, u32[]{:S(2)}) copy-start(bf16[96,2,1280]{2,0,1:T(8,128)(2,1)} %copy-done.15) | copy-start | bytes 1474564
  343.0 21.9 %copy-start.20 = (bf16[48,2,1280]{2,0,1:T(8,128)(2,1)S(1)}, bf16[48,2,1280]{2,0,1:T(8,128)(2,1)}, u32[]{:S(2)}) copy-start(bf16[48,2,1280]{2,0,1:T(8,128)(2,1)} %copy-done.18) | copy-start | bytes 737284
  346.6 101.6 %collective-permute-start.5 = (bf16[384,2,1280]{0,2,1:T(8,128)(2,1)}, bf16[384,2,1280]{0,2,1:T(8,128)(2,1)}, u32[]{:S(2)}, u32[]{:S(2)}) collective-permute-start(bf16[384,2,1280]{0,2,1:T(8,128)(2,1)} %pad_maximum_fusion.4), channel_id=1, source_target_pairs={{0,4},{4,0},{1,5},{5,1},{2,6},{6,2},{3,7},{7,3},{8,12},{12,8},{9,1... | collective-permute-start | bytes 5898248 | tf_op jit(solution)/shard_map/ppermute | solution.py:14
  367.6 91.4 %collective-permute-start.9 = (bf16[384,2,1280]{2,0,1:T(8,128)(2,1)}, bf16[384,2,1280]{2,0,1:T(8,128)(2,1)}, u32[]{:S(2)}, u32[]{:S(2)}) collective-permute-start(bf16[384,2,1280]{2,0,1:T(8,128)(2,1)} %pad_maximum_fusion.5), channel_id=1, source_target_pairs={{0,8},{8,0},{1,9},{9,1},{2,10},{10,2},{3,11},{11,3},{4,12},{12,4},... | collective-permute-start | bytes 5898248 | tf_op jit(solution)/shard_map/ppermute | solution.py:14
  372.5 3.5 copy-start.17
  377.9 4.4 copy-start.2
  377.9 26.7 %copy-start.7 = (bf16[192,2,1280]{0,2,1:T(8,128)(2,1)S(1)}, bf16[192,2,1280]{0,2,1:T(8,128)(2,1)}, u32[]{:S(2)}) copy-start(bf16[192,2,1280]{0,2,1:T(8,128)(2,1)} %copy-done.6) | copy-start | bytes 2949124
  407.4 1.1 copy-start.21
  415.5 32.7 %copy-start.9 = (bf16[96,2,1280]{0,2,1:T(8,128)(2,1)S(1)}, bf16[96,2,1280]{0,2,1:T(8,128)(2,1)}, u32[]{:S(2)}) copy-start(bf16[96,2,1280]{0,2,1:T(8,128)(2,1)} %copy-done.8) | copy-start | bytes 1474564
  451.7 1.0 copy-start.23
  469.1 4.1 copy-start.24
  473.2 1.5 copy-start.22
  478.0 7.8 %copy-start.10 = (f32[384,1280]{0,1:T(8,128)S(1)}, f32[384,1280]{0,1:T(8,128)}, u32[]{:S(2)}) copy-start(f32[384,1280]{0,1:T(8,128)} %copy.86) | copy-start | bytes 5898244
  478.0 7.8 %copy-start.11 = (f32[384,1280]{0,1:T(8,128)S(1)}, f32[384,1280]{0,1:T(8,128)}, u32[]{:S(2)}) copy-start(f32[384,1280]{0,1:T(8,128)} %copy.103) | copy-start | bytes 5898244
  478.0 7.8 %copy-start.12 = (f32[384,1280]{0,1:T(8,128)S(1)}, f32[384,1280]{0,1:T(8,128)}, u32[]{:S(2)}) copy-start(f32[384,1280]{0,1:T(8,128)} %copy.111) | copy-start | bytes 5898244
  486.9 7.0 %copy-start.1 = (bf16[1,384,2560]{2,1,0:T(8,128)(2,1)S(1)}, bf16[1,384,2560]{2,1,0:T(8,128)(2,1)}, u32[]{:S(2)}) copy-start(bf16[1,384,2560]{2,1,0:T(8,128)(2,1)} %param.4) | copy-start | bytes 5898244
Sparse Core Ops, SparseCore 0:
  9.0 237.9 all-gather.2
  248.6 86.8 all-gather.4
where the time goes:
time: 510 us; the launch traced here: 501 us
  waiting for transfers between devices  322 us (63%)
  local copies, waits for them, and re-layouts  65.4 us (13%)
  other arithmetic  51 us (10%)
  matrix products  35.1 us (7%)
  between operations  14.2 us (3%)
  starting transfers between devices  13.2 us (3%)
    all_gather x1, waiting for transfers between devices, local(): lax.all_gather(qkv_weight, 'dp', axis=1, tiled=True)  238 us
    ppermute x10, waiting for transfers between devices, from_partner(): return lax.ppermute(block, axis, route)  82.6 us
    concatenate x9, other arithmetic, local(): gathered = jnp.concatenate([gathered, partner], axis=0)  22.4 us
    reduce_sum x6, other arithmetic, select_rows(): jnp.sum(jnp.where(table, grouped, jnp.zeros((), grouped.dtype)), axis=1)  18.9 us
    ppermute x10, starting transfers between devices, from_partner(): return lax.ppermute(block, axis, route)  13.2 us
    dot_general x1, matrix products, local(): jnp.dot(token_flat, lax.all_gather(qkv_weight, 'dp', axis=1, tiled=True),...  12.3 us
    unnamed x65, local copies, waits for them, and re-layouts  12.3 us
    dot_general x4, matrix products, attend(): jnp.einsum('hqk,khd->qhd', expo.astype(jnp.bfloat16), value_rows, preferr...  11.6 us
  transfers between devices with their start and end apart: 12, of which 6 were waited for; matrix products, arithmetic and copies ran while one was open for 28% of the time, Pallas kernels for 0%

commit v1 on v0

--- a/solution.py
+++ b/solution.py
@@ -49,7 +49,9 @@
     token_flat = tokens.reshape(tok_rows, tokens.shape[2])
     projected = jnp.dot(
         token_flat,
-        lax.all_gather(qkv_weight, "dp", axis=1, tiled=True),
+        jnp.concatenate(
+            lax.all_to_all(jnp.stack([qkv_weight] * lax.axis_size("dp")), "dp", 0, 0), axis=1
+        ),
         preferred_element_type=jnp.float32,
     ).astype(jnp.bfloat16)
     all_query = projected[:, :inner_width].reshape(tok_rows, head_count, head_size)

time: 510 us -> 601 us (1.18)
  waiting for transfers between devices: 322 us -> 362 us
  local copies, waits for them, and re-layouts: 65.4 us -> 83.7 us
  other arithmetic: 51 us -> 67.6 us
  starting transfers between devices: 13.2 us -> 26.1 us
    all_to_all x0 -> x1, waiting for transfers between devices: none -> 281 us  [local(): lax.all_to_all(jnp.stack([qkv_weight] * lax.axis_size('dp')), 'dp', 0, 0)]
    all_gather x1 -> x0, waiting for transfers between devices: 238 us -> none  [local(): lax.all_gather(qkv_weight, 'dp', axis=1, tiled=True)]
    another operation x0 -> x1, other arithmetic: none -> 16.9 us  [local(): jnp.stack([qkv_weight] * lax.axis_size('dp'))]
    unnamed x65 -> x62, local copies, waits for them, and re-layouts: 12.3 us -> 25.1 us
    all_to_all x0 -> x1, starting transfers between devices: none -> 10.7 us  [local(): lax.all_to_all(jnp.stack([qkv_weight] * lax.axis_size('dp')), 'dp', 0, 0)]
  transfers between devices with their start and end apart: 12 -> 12, of which waited for: 6 -> 6; matrix products, arithmetic and copies ran while one was open for 28% -> 25% of each run, Pallas kernels for 0% -> 0%
where the time goes in v1:
time: 601 us; the launch traced here: 591 us
  waiting for transfers between devices  362 us (60%)
  local copies, waits for them, and re-layouts  83.7 us (14%)
  other arithmetic  67.6 us (11%)
  matrix products  37.2 us (6%)
  starting transfers between devices  26.1 us (4%)
  between operations  14.4 us (2%)
    all_to_all x1, waiting for transfers between devices, local(): lax.all_to_all(jnp.stack([qkv_weight] * lax.axis_size('dp')), 'dp', 0, 0)  281 us
    ppermute x10, waiting for transfers between devices, from_partner(): return lax.ppermute(block, axis, route)  80.2 us
    unnamed x62, local copies, waits for them, and re-layouts  25.1 us
    concatenate x9, other arithmetic, local(): gathered = jnp.concatenate([gathered, partner], axis=0)  22 us
    reduce_sum x6, other arithmetic, select_rows(): jnp.sum(jnp.where(table, grouped, jnp.zeros((), grouped.dtype)), axis=1)  19 us
    another operation x1, other arithmetic, local(): jnp.stack([qkv_weight] * lax.axis_size('dp'))  16.9 us
    ppermute x10, starting transfers between devices, from_partner(): return lax.ppermute(block, axis, route)  15.4 us
    dot_general x1, matrix products, local(): jnp.dot(token_flat, jnp.concatenate(lax.all_to_all(jnp.stack([qkv_weight]...  14.4 us
  transfers between devices with their start and end apart: 12, of which 6 were waited for; matrix products, arithmetic and copies ran while one was open for 25% of the time, Pallas kernels for 0%

profile of v1, /device:TPU:0, one launch (start us, length us, event | category | flops | bytes accessed | tf_op | source)
XLA Modules:
  0.0 591.2 jit_solution(15006677268361344178)
XLA Ops:
  6.5 13.7 %copy.76 = bf16[2560,1920]{0,1:T(8,128)(2,1)} copy(bf16[2560,1920]{1,0:T(8,128)(2,1)} %param.5) | data formatting | bytes 19660800 | tf_op args[1]
  20.3 16.9 %pad_maximum_fusion = bf16[2,2560,1920]{1,2,0:T(8,128)(2,1)} fusion(bf16[1,2560,1920]{1,2,0:T(8,128)(2,1)} %bitcast.149), kind=kLoop, calls=%fused_computation | loop fusion | flops 9830400 | bytes 29491200 | tf_op jit(solution)/shard_map/stack | solution.py:53
  37.2 10.7 %all-to-all-start = ((bf16[2,2560,1920]{1,2,0:T(8,128)(2,1)}), bf16[2,2560,1920]{1,2,0:T(8,128)(2,1)}, u32[]{:S(2)}, u32[]{:S(2)}) async-start(bf16[2,2560,1920]{1,2,0:T(8,128)(2,1)} %pad_maximum_fusion), calls=%async_computation | async-start | bytes 39321600 | tf_op jit(solution)/shard_map/all_to_all | solution.py:53
  50.1 281.4 %all-to-all-done = bf16[2,2560,1920]{1,2,0:T(8,128)(2,1)} async-done(((bf16[2,2560,1920]{1,2,0:T(8,128)(2,1)}), bf16[2,2560,1920]{1,2,0:T(8,128)(2,1)}, u32[]{:S(2)}, u32[]{:S(2)}) %all-to-all-start) | async-done | bytes 19660832 | tf_op jit(solution)/shard_map/all_to_all | solution.py:53
  331.4 14.4 %fusion.6 = bf16[384,3840]{0,1:T(8,128)(2,1)S(1)} fusion(bf16[2560,3840]{0,1:T(8,128)(2,1)} %bitcast.4, bf16[1,384,2560]{2,1,0:T(8,128)(2,1)S(1)} %copy-done), kind=kOutput, calls=%fused_computation.11 | convolution fusion | flops 7551221760 | bytes 24576000 | tf_op jit(solution)/shard_map/dot_general | solution.py:50
  348.5 2.7 copy.80
  351.2 2.7 reshape_reshape.27
  353.9 2.7 reshape_reshape.29
  356.6 4.9 select_reduce_fusion.1
  361.5 2.0 copy.81
  365.0 2.3 copy.79
  367.3 3.2 reshape_reshape.26
  370.5 3.3 select_reduce_fusion.4
  373.8 4.2 select_reduce_fusion
  378.0 2.6 copy.96
  380.6 2.1 copy.97
  383.2 2.1 select_reduce_fusion.2
  387.1 3.2 broadcast_select_fusion
  394.8 2.1 collective-permute-start.7
  396.9 2.9 select_reduce_fusion.3
  402.9 2.3 copy.99
  405.2 4.0 collective-permute-done.7
  409.2 2.2 pad_maximum_fusion.8
  411.4 3.9 collective-permute-start.8
  418.4 2.0 pad_maximum_fusion.4
  421.5 8.8 %collective-permute-done.4 = bf16[192,2,1280]{2,0,1:T(8,128)(2,1)} collective-permute-done((bf16[192,2,1280]{2,0,1:T(8,128)(2,1)}, bf16[192,2,1280]{2,0,1:T(8,128)(2,1)}, u32[]{:S(2)}, u32[]{:S(2)}) %collective-permute-start.4) | collective-permute-done | bytes 983072 | tf_op jit(solution)/shard_map/ppermute | solution.py:14
  431.9 3.5 pad_maximum_fusion.5
  435.5 3.9 collective-permute-start.5
  439.4 15.6 %collective-permute-done.8 = bf16[192,2,1280]{2,0,1:T(8,128)(2,1)} collective-permute-done((bf16[192,2,1280]{2,0,1:T(8,128)(2,1)}, bf16[192,2,1280]{2,0,1:T(8,128)(2,1)}, u32[]{:S(2)}, u32[]{:S(2)}) %collective-permute-start.8) | collective-permute-done | bytes 983072 | tf_op jit(solution)/shard_map/ppermute | solution.py:14
  455.0 2.7 pad_maximum_fusion.6
  457.7 3.2 collective-permute-start.9
  460.9 2.2 constant_dynamic-update-slice_fusion.1
  463.1 2.9 pad_maximum_fusion.3
  466.0 1.9 multiply_reduce_fusion
  468.0 2.7 fusion
  472.4 21.2 %collective-permute-done.2 = bf16[384,2,1280]{0,2,1:T(8,128)(2,1)} collective-permute-done((bf16[384,2,1280]{0,2,1:T(8,128)(2,1)}, bf16[384,2,1280]{0,2,1:T(8,128)(2,1)}, u32[]{:S(2)}, u32[]{:S(2)}) %collective-permute-start.2) | collective-permute-done | bytes 1966112 | tf_op jit(solution)/shard_map/ppermute | solution.py:14
  493.6 2.7 pad_maximum_fusion.1
  502.2 2.2 copy.151
  504.5 3.0 copy.93
  507.8 30.5 %collective-permute-done.5 = bf16[384,2,1280]{0,2,1:T(8,128)(2,1)} collective-permute-done((bf16[384,2,1280]{0,2,1:T(8,128)(2,1)}, bf16[384,2,1280]{0,2,1:T(8,128)(2,1)}, u32[]{:S(2)}, u32[]{:S(2)}) %collective-permute-start.5) | collective-permute-done | bytes 1966112 | tf_op jit(solution)/shard_map/ppermute | solution.py:14
  538.3 3.5 pad_maximum_fusion.2
  549.1 3.0 constant_dynamic-update-slice_fusion
  552.0 4.3 fusion.68
  556.3 2.7 copy.116
  559.0 4.1 copy.119
  565.7 1.9 copy.122
  568.0 7.8 %fusion.22 = f32[384,10,128]{0,2,1:T(8,128)S(1)} fusion(bf16[768,10,128]{0,2,1:T(8,128)(2,1)} %bitcast.169, f32[10,384,768]{2,1,0:T(8,128)} %copy-done.2, f32[10,384]{1,0:T(8,128)S(1)} %get-tuple-element.25, f32[384,10]{0,1:T(8,128)S(1)} %get-tuple-element.11, f32[384,10]{0,1:T(8,128)S(1)} %bitcast.175, pred[10]{0:T(512)(128)(4,1)S(1)} %copy-done.24), kind=kOutput, calls=%fused_computation.48 | convolution fusion | flops 765296640 | bytes 15774730 | tf_op jit(solution)/shard_map/hqk,khd->qhd/dot_general | solution.py:37
  576.9 7.0 %fusion.9 = bf16[1,384,2560]{2,1,0:T(8,128)(2,1)} fusion(bf16[384,1280]{0,1:T(8,128)(2,1)S(1)} %fusion.17, bf16[1280,2560]{1,0:T(8,128)(2,1)} %all-gather.2.cloned.1.call-done), kind=kOutput, calls=%fused_computation.19 | convolution fusion | flops 2517565440 | bytes 9502720 | tf_op jit(solution)/shard_map/dot_general | solution.py:100
  (129 shorter events, 40.9 us)
Async XLA Ops:
  6.5 324.9 %copy-start = (bf16[1,384,2560]{2,1,0:T(8,128)(2,1)S(1)}, bf16[1,384,2560]{2,1,0:T(8,128)(2,1)}, u32[]{:S(2)}) copy-start(bf16[1,384,2560]{2,1,0:T(8,128)(2,1)} %param.4) | copy-start | bytes 5898244
  37.2 294.2 %all-to-all-start = ((bf16[2,2560,1920]{1,2,0:T(8,128)(2,1)}), bf16[2,2560,1920]{1,2,0:T(8,128)(2,1)}, u32[]{:S(2)}, u32[]{:S(2)}) async-start(bf16[2,2560,1920]{1,2,0:T(8,128)(2,1)} %pad_maximum_fusion), calls=%async_computation | async-start | bytes 39321600 | tf_op jit(solution)/shard_map/all_to_all | solution.py:53
  47.9 0.8 copy-start.27
  47.9 529.0 %all-gather.2.cloned.1.call-start = ((), (), s32[]{:S(2)}) async-start(), calls=%async_computation.1 | async-start | bytes 9830400 | tf_op jit(solution)/shard_map/all_gather | solution.py:102
  49.3 324.5 %copy-start.25 = (pred[4,10]{1,0:T(4,128)(4,1)}, pred[4,10]{1,0:T(4,128)(4,1)S(1)}, u32[]{:S(2)}) copy-start(pred[4,10]{1,0:T(4,128)(4,1)S(1)} %iota_compare_fusion.1) | copy-start | bytes 124
  49.5 0.5 copy-start.23
  364.9 52.0 %collective-permute-start.1 = (bf16[192,2,1280]{2,0,1:T(8,128)(2,1)}, bf16[192,2,1280]{2,0,1:T(8,128)(2,1)}, u32[]{:S(2)}, u32[]{:S(2)}) collective-permute-start(bf16[192,2,1280]{2,0,1:T(8,128)(2,1)} %copy.82), channel_id=1, source_target_pairs={{0,1},{1,0},{2,3},{3,2},{4,5},{5,4},{6,7},{7,6},{8,9},{9,8},{10,11... | collective-permute-start | bytes 2949128 | tf_op jit(solution)/shard_map/ppermute | solution.py:14
  382.7 17.2 %collective-permute-start.3 = (bf16[96,2,1280]{2,0,1:T(8,128)(2,1)}, bf16[96,2,1280]{2,0,1:T(8,128)(2,1)}, u32[]{:S(2)}, u32[]{:S(2)}) collective-permute-start(bf16[96,2,1280]{2,0,1:T(8,128)(2,1)} %copy.97), channel_id=1, source_target_pairs={{0,1},{1,0},{2,3},{3,2},{4,5},{5,4},{6,7},{7,6},{8,9},{9,8},{10,11... | collective-permute-start | bytes 1474568 | tf_op jit(solution)/shard_map/ppermute | solution.py:14
  387.1 6.8 %collective-permute-start.6 = (bf16[48,2,1280]{2,0,1:T(8,128)(2,1)S(1)}, bf16[48,2,1280]{2,0,1:T(8,128)(2,1)S(1)}, u32[]{:S(2)}, u32[]{:S(2)}) collective-permute-start(bf16[48,2,1280]{2,0,1:T(8,128)(2,1)S(1)} %get-tuple-element.20), channel_id=1, source_target_pairs={{0,1},{1,0},{2,3},{3,2},{4,5},{5,4},{6,7},{7,6},{8,9},{9,8},{10,11... | collective-permute-start | bytes 737288 | tf_op jit(solution)/shard_map/ppermute | solution.py:14
  387.1 3.2 copy-start.4
  391.9 5.0 copy-start.26
  393.4 7.8 %copy-start.3 = (bf16[96,2,10,128]{0,3,2,1:T(8,128)(2,1)S(1)}, bf16[96,2,10,128]{0,3,2,1:T(8,128)(2,1)}, u32[]{:S(2)}) copy-start(bf16[96,2,10,128]{0,3,2,1:T(8,128)(2,1)} %copy.96) | copy-start | bytes 1474564
  393.4 69.7 %collective-permute-start = (bf16[384,2,1280]{0,2,1:T(8,128)(2,1)}, bf16[384,2,1280]{0,2,1:T(8,128)(2,1)}, u32[]{:S(2)}, u32[]{:S(2)}) collective-permute-start(bf16[384,2,1280]{0,2,1:T(8,128)(2,1)} %broadcast_select_fusion), channel_id=1, source_target_pairs={{0,1},{1,0},{2,3},{3,2},{4,5},{5,4},{6,7},{7,6},{8,9},{9,8},{10,11... | collective-permute-start | bytes 5898248 | tf_op jit(solution)/shard_map/ppermute | solution.py:14
  393.9 5.9 %copy-start.16 = (bf16[48,2,1280]{2,0,1:T(8,128)(2,1)}, bf16[48,2,1280]{2,0,1:T(8,128)(2,1)S(1)}, u32[]{:S(2)}) copy-start(bf16[48,2,1280]{2,0,1:T(8,128)(2,1)S(1)} %collective-permute-done.6) | copy-start | bytes 737284
  394.8 14.4 %collective-permute-start.7 = (bf16[96,2,1280]{2,0,1:T(8,128)(2,1)}, bf16[96,2,1280]{2,0,1:T(8,128)(2,1)S(1)}, u32[]{:S(2)}, u32[]{:S(2)}) collective-permute-start(bf16[96,2,1280]{2,0,1:T(8,128)(2,1)} %pad_maximum_fusion.9), channel_id=1, source_target_pairs={{0,2},{2,0},{1,3},{3,1},{4,6},{6,4},{5,7},{7,5},{8,10},{10,8},{9,1... | collective-permute-start | bytes 1474568 | tf_op jit(solution)/shard_map/ppermute | solution.py:14
  401.2 4.0 copy-start.7
  405.2 10.1 %copy-start.17 = (bf16[48,2,1280]{2,0,1:T(8,128)(2,1)S(1)}, bf16[48,2,1280]{2,0,1:T(8,128)(2,1)}, u32[]{:S(2)}) copy-start(bf16[48,2,1280]{2,0,1:T(8,128)(2,1)} %copy-done.16) | copy-start | bytes 737284
  405.2 25.2 %collective-permute-start.4 = (bf16[192,2,1280]{2,0,1:T(8,128)(2,1)}, bf16[192,2,1280]{2,0,1:T(8,128)(2,1)}, u32[]{:S(2)}, u32[]{:S(2)}) collective-permute-start(bf16[192,2,1280]{2,0,1:T(8,128)(2,1)} %copy.99), channel_id=1, source_target_pairs={{0,2},{2,0},{1,3},{3,1},{4,6},{6,4},{5,7},{7,5},{8,10},{10,8},{9,1... | collective-permute-start | bytes 2949128 | tf_op jit(solution)/shard_map/ppermute | solution.py:14
  409.2 7.6 %copy-start.14 = (bf16[96,2,1280]{2,0,1:T(8,128)(2,1)}, bf16[96,2,1280]{2,0,1:T(8,128)(2,1)S(1)}, u32[]{:S(2)}) copy-start(bf16[96,2,1280]{2,0,1:T(8,128)(2,1)S(1)} %collective-permute-done.7) | copy-start | bytes 1474564
  411.4 43.6 %collective-permute-start.8 = (bf16[192,2,1280]{2,0,1:T(8,128)(2,1)}, bf16[192,2,1280]{2,0,1:T(8,128)(2,1)}, u32[]{:S(2)}, u32[]{:S(2)}) collective-permute-start(bf16[192,2,1280]{2,0,1:T(8,128)(2,1)} %pad_maximum_fusion.8), channel_id=1, source_target_pairs={{0,4},{4,0},{1,5},{5,1},{2,6},{6,2},{3,7},{7,3},{8,12},{12,8},{9,1... | collective-permute-start | bytes 2949128 | tf_op jit(solution)/shard_map/ppermute | solution.py:14
  418.4 2.0 copy-start.5
  420.4 73.1 %collective-permute-start.2 = (bf16[384,2,1280]{0,2,1:T(8,128)(2,1)}, bf16[384,2,1280]{0,2,1:T(8,128)(2,1)}, u32[]{:S(2)}, u32[]{:S(2)}) collective-permute-start(bf16[384,2,1280]{0,2,1:T(8,128)(2,1)} %pad_maximum_fusion.4), channel_id=1, source_target_pairs={{0,2},{2,0},{1,3},{3,1},{4,6},{6,4},{5,7},{7,5},{8,10},{10,8},{9,1... | collective-permute-start | bytes 5898248 | tf_op jit(solution)/shard_map/ppermute | solution.py:14
  431.9 23.1 %copy-start.15 = (bf16[96,2,1280]{2,0,1:T(8,128)(2,1)S(1)}, bf16[96,2,1280]{2,0,1:T(8,128)(2,1)}, u32[]{:S(2)}) copy-start(bf16[96,2,1280]{2,0,1:T(8,128)(2,1)} %copy-done.14) | copy-start | bytes 1474564
  431.9 23.1 %copy-start.18 = (bf16[48,2,1280]{2,0,1:T(8,128)(2,1)S(1)}, bf16[48,2,1280]{2,0,1:T(8,128)(2,1)}, u32[]{:S(2)}) copy-start(bf16[48,2,1280]{2,0,1:T(8,128)(2,1)} %copy-done.16) | copy-start | bytes 737284
  435.5 102.8 %collective-permute-start.5 = (bf16[384,2,1280]{0,2,1:T(8,128)(2,1)}, bf16[384,2,1280]{0,2,1:T(8,128)(2,1)}, u32[]{:S(2)}, u32[]{:S(2)}) collective-permute-start(bf16[384,2,1280]{0,2,1:T(8,128)(2,1)} %pad_maximum_fusion.5), channel_id=1, source_target_pairs={{0,4},{4,0},{1,5},{5,1},{2,6},{6,2},{3,7},{7,3},{8,12},{12,8},{9,1... | collective-permute-start | bytes 5898248 | tf_op jit(solution)/shard_map/ppermute | solution.py:14
  457.7 5.4 copy-start.13
  457.7 91.4 %collective-permute-start.9 = (bf16[384,2,1280]{2,0,1:T(8,128)(2,1)}, bf16[384,2,1280]{2,0,1:T(8,128)(2,1)}, u32[]{:S(2)}, u32[]{:S(2)}) collective-permute-start(bf16[384,2,1280]{2,0,1:T(8,128)(2,1)} %pad_maximum_fusion.6), channel_id=1, source_target_pairs={{0,8},{8,0},{1,9},{9,1},{2,10},{10,2},{3,11},{11,3},{4,12},{12,4},... | collective-permute-start | bytes 5898248 | tf_op jit(solution)/shard_map/ppermute | solution.py:14
  463.1 2.9 copy-start.9
  463.1 2.9 copy-start.24
  468.0 4.4 copy-start.2
  468.0 25.6 %copy-start.6 = (bf16[192,2,1280]{0,2,1:T(8,128)(2,1)S(1)}, bf16[192,2,1280]{0,2,1:T(8,128)(2,1)}, u32[]{:S(2)}) copy-start(bf16[192,2,1280]{0,2,1:T(8,128)(2,1)} %copy-done.5) | copy-start | bytes 2949124
  496.2 1.1 copy-start.19
  504.5 33.8 %copy-start.8 = (bf16[96,2,1280]{0,2,1:T(8,128)(2,1)S(1)}, bf16[96,2,1280]{0,2,1:T(8,128)(2,1)}, u32[]{:S(2)}) copy-start(bf16[96,2,1280]{0,2,1:T(8,128)(2,1)} %copy-done.7) | copy-start | bytes 1474564
  541.8 1.0 copy-start.21
  559.0 4.1 copy-start.22
  563.1 1.5 copy-start.20
  568.0 7.8 %copy-start.10 = (f32[384,1280]{0,1:T(8,128)S(1)}, f32[384,1280]{0,1:T(8,128)}, u32[]{:S(2)}) copy-start(f32[384,1280]{0,1:T(8,128)} %copy.93) | copy-start | bytes 5898244
  568.0 7.8 %copy-start.11 = (f32[384,1280]{0,1:T(8,128)S(1)}, f32[384,1280]{0,1:T(8,128)}, u32[]{:S(2)}) copy-start(f32[384,1280]{0,1:T(8,128)} %copy.112) | copy-start | bytes 5898244
  568.0 7.8 %copy-start.12 = (f32[384,1280]{0,1:T(8,128)S(1)}, f32[384,1280]{0,1:T(8,128)}, u32[]{:S(2)}) copy-start(f32[384,1280]{0,1:T(8,128)} %copy.122) | copy-start | bytes 5898244
  576.9 7.0 %copy-start.1 = (bf16[1,384,2560]{2,1,0:T(8,128)(2,1)S(1)}, bf16[1,384,2560]{2,1,0:T(8,128)(2,1)}, u32[]{:S(2)}) copy-start(bf16[1,384,2560]{2,1,0:T(8,128)(2,1)} %param.4) | copy-start | bytes 5898244
Sparse Core Ops, SparseCore 0:
  50.4 159.1 all-gather.1
